TPU v7x, 32 devices: a whole 2x2x4 slice. The times are simulated.
32 devices in a mesh: expert: 8 (over y, x, core), tensor: 4 (over z).
Axes of the slice: x: 2, y: 2, z: 4, core: 2. Of those that a mesh axis runs over, the one named last changes fastest.
Arguments:
- tokens: bfloat16 [8192, 1024], P('expert'), may hold values from -6 to 6
- cotangent: bfloat16 [8192, 1024], P('expert'), may hold values from -6 to 6
- routes: int32 [8192], P('expert'), may hold values from 0 to 15, as said below
- slot_index: int32 [8192], P('expert'), may hold values from 0 to 128, as said below
- first_gain: float32 [1024], replicated, may hold values from 0.1 to 1.9
- first_shift: float32 [1024], replicated, may hold values from -1.25 to 1.25
- project_in: bfloat16 [1024, 3, 1024], P(None, None, 'tensor'), may hold values from -0.25 to 0.25
- project_out: bfloat16 [1024, 1024], P('tensor'), may hold values from -1.5 to 1.5
- second_gain: float32 [1024], replicated, may hold values from 0.1 to 1.9
- second_shift: float32 [1024], replicated, may hold values from -1.25 to 1.25
- router_weight: bfloat16 [1024, 16], replicated, may hold values from -0.09375 to 0.09375
- mixing_weight: bfloat16 [1024, 2], replicated, may hold values from -0.1875 to 0.1875
- dense_up: bfloat16 [1024, 4096], P(None, 'tensor'), may hold values from -0.1875 to 0.1875
- dense_down: bfloat16 [4096, 1024], P('tensor'), may hold values from -0.1875 to 0.1875
- expert_up: bfloat16 [16, 1024, 4096], P('expert', None, 'tensor'), may hold values from -0.375 to 0.375
- expert_down: bfloat16 [16, 4096, 1024], P('expert', 'tensor'), may hold values from -3 to 3
Outputs:
- layer_out: bfloat16 [8192, 1024], P('expert')
- input_grad: bfloat16 [8192, 1024], P('expert')
- first_gain_grad: float32 [1024], replicated
- first_shift_grad: float32 [1024], replicated
- project_in_grad: float32 [1024, 3, 1024], P(None, None, 'tensor')
- project_out_grad: float32 [1024, 1024], P('tensor')
- second_gain_grad: float32 [1024], replicated
- second_shift_grad: float32 [1024], replicated
- router_grad: float32 [1024, 16], replicated
- mixing_grad: float32 [1024, 2], replicated
- dense_up_grad: float32 [1024, 4096], P(None, 'tensor')
- dense_down_grad: float32 [4096, 1024], P('tensor')
- expert_up_grad: float32 [16, 1024, 4096], P('expert', None, 'tensor')
- expert_down_grad: float32 [16, 4096, 1024], P('expert', 'tensor')
Inputs may be any that keep to these rules, and one draw needn't show every extreme that they name: `routes`: in every block of 1024 tokens (tokens b * 1024 to (b + 1) * 1024 - 1) some expert is named by more than 128 tokens. slot_index[t] is the number of earlier tokens of t's block with the same route, or 128 where that number is 128 or more (the token is dropped); so at most 128 kept tokens of a block name one expert, and every block fills all 128 slots of some expert.
All inputs are finite; a program needn't handle non-finite values.
Results may differ from a plain program's by a relative error of at most 0.023.
Values may be sent and summed in bfloat16 or wider, within the bound.
No kernel may reach another device: no remote copies, remote signals or barrier semaphores. Data moves between devices by JAX's collectives and lax.ppermute only.
A program may use at most 192 MiB of HBM per device.

v0:
```python
import jax
import jax.numpy as jnp
from jax import lax
from jax.sharding import PartitionSpec as P

HEAD_DIM = 64
SEQ = 1024
EPS = 1e-05
NEGATIVE = -1e30


def layer_norm(row_values, norm_gain, norm_shift):
    row_mean = jnp.mean(row_values, axis=-1, keepdims=True)
    centred = row_values - row_mean
    spread = jnp.mean(centred * centred, axis=-1, keepdims=True)
    return centred * lax.rsqrt(spread + EPS) * norm_gain + norm_shift


def gelu_tanh(values):
    return jax.nn.gelu(values, approximate=True)


def gelu_back(pre_act, incoming):
    return jax.vjp(gelu_tanh, pre_act)[1](incoming)[0]


def causal_scores(query_block, key_seq, offset):
    score_scale = HEAD_DIM ** (-0.5)
    scores = (
        jnp.einsum("qhd,khd->hqk", query_block, key_seq, preferred_element_type=jnp.float32)
        * score_scale
    )
    query_pos = offset + lax.iota(jnp.int32, query_block.shape[0])
    key_pos = lax.iota(jnp.int32, key_seq.shape[0])
    allowed = key_pos[None, :] <= query_pos[:, None]
    return jnp.where(allowed[None], scores, NEGATIVE)


def attend_forward(queries, key_rows, values, block_rows):
    row_count, head_count, head_width = queries.shape
    per_seq = SEQ // block_rows

    def one_block(block_index):
        seq_start = block_index // per_seq * SEQ
        offset = block_index % per_seq * block_rows
        query_block = lax.dynamic_slice_in_dim(queries, seq_start + offset, block_rows, 0)
        scores = causal_scores(query_block, key_rows, offset)
        row_max = jnp.max(scores, axis=-1, keepdims=True)
        powers = jnp.exp(scores - row_max)
        row_total = jnp.sum(powers, axis=-1, keepdims=True)
        weights = (powers / row_total).astype(jnp.bfloat16)
        blended = jnp.einsum("hqk,khd->qhd", weights, values, preferred_element_type=jnp.float32)
        return (blended.astype(jnp.bfloat16), (row_max + jnp.log(row_total))[..., 0])

    blended, log_total = lax.map(one_block, jnp.arange(row_count // block_rows, dtype=jnp.int32))
    return (blended.reshape(row_count, head_count * head_width), log_total)


def attend_backward(queries, key_rows, values, log_total, grad_blended, block_rows):
    row_count, head_count, head_width = queries.shape
    per_seq = SEQ // block_rows
    score_scale = HEAD_DIM ** (-0.5)

    def one_seq(sequence):
        seq_start = sequence * SEQ

        def step(totals, inner_index):
            key_acc, value_acc = totals
            offset = inner_index * block_rows
            query_block = lax.dynamic_slice_in_dim(queries, seq_start + offset, block_rows, 0)
            grad_block = lax.dynamic_slice_in_dim(grad_blended, seq_start + offset, block_rows, 0)
            row_log = lax.dynamic_index_in_dim(
                log_total, sequence * per_seq + inner_index, 0, keepdims=False
            )
            scores = causal_scores(query_block, key_rows, offset)
            weights = jnp.exp(scores - row_log[..., None])
            weight_grad = jnp.einsum(
                "qhd,khd->hqk", grad_block, values, preferred_element_type=jnp.float32
            )
            row_inner = jnp.sum(weights * weight_grad, axis=-1, keepdims=True)
            score_grad = (weights * (weight_grad - row_inner)).astype(jnp.bfloat16)
            query_grad = (
                jnp.einsum("hqk,khd->qhd", score_grad, key_rows, preferred_element_type=jnp.float32)
                * score_scale
            )
            key_acc = (
                key_acc
                + jnp.einsum(
                    "hqk,qhd->khd", score_grad, query_block, preferred_element_type=jnp.float32
                )
                * score_scale
            )
            value_acc = value_acc + jnp.einsum(
                "hqk,qhd->khd",
                weights.astype(jnp.bfloat16),
                grad_block,
                preferred_element_type=jnp.float32,
            )
            return ((key_acc, value_acc), query_grad)

        empty_acc = jnp.zeros((SEQ, head_count, head_width), jnp.float32)
        (key_grad, value_grad), query_grad = lax.scan(
            step, (empty_acc, empty_acc), jnp.arange(per_seq, dtype=jnp.int32)
        )
        return (query_grad.reshape(SEQ, head_count, head_width), key_grad, value_grad)

    query_grad, key_grad, value_grad = lax.map(
        one_seq, jnp.arange(row_count // SEQ, dtype=jnp.int32)
    )
    flat_width = head_count * head_width
    return jnp.stack(
        [
            query_grad.reshape(row_count, flat_width),
            key_grad.reshape(row_count, flat_width),
            value_grad.reshape(row_count, flat_width),
        ],
        axis=1,
    )


def send_home(buffer):
    return lax.all_to_all(
        buffer.astype(jnp.bfloat16), "expert", split_axis=1, concat_axis=0, tiled=True
    ).astype(buffer.dtype)


def send_grads_home(buffer):
    return lax.all_to_all(
        buffer.astype(jnp.bfloat16), "expert", split_axis=1, concat_axis=0, tiled=True
    ).astype(buffer.dtype)


def local(
    tokens,
    cotangent,
    routes,
    slot_index,
    first_gain,
    first_shift,
    project_in,
    project_out,
    second_gain,
    second_shift,
    router_weight,
    mixing_weight,
    dense_up,
    dense_down,
    expert_up,
    expert_down,
):
    inputs = tokens.astype(jnp.float32)
    cotan_rows = cotangent.astype(jnp.float32)
    row_count, model_width = inputs.shape
    expert_count = router_weight.shape[1]
    capacity = 2 * row_count // expert_count
    head_count = project_in.shape[2] // HEAD_DIM
    block_rows = min(512, SEQ)
    normed_in, first_back = jax.vjp(layer_norm, inputs, first_gain, first_shift)
    normed_low = normed_in.astype(jnp.bfloat16)
    projected = jnp.einsum(
        "td,dcn->tcn", normed_low, project_in, preferred_element_type=jnp.float32
    ).astype(jnp.bfloat16)
    queries = projected[:, 0].reshape(row_count, head_count, HEAD_DIM)
    key_rows = projected[:, 1].reshape(row_count, head_count, HEAD_DIM)
    values = projected[:, 2].reshape(row_count, head_count, HEAD_DIM)
    attended, log_total = attend_forward(queries, key_rows, values, block_rows)
    attn_part = jnp.dot(attended, project_out, preferred_element_type=jnp.float32)
    attn_full = lax.psum(attn_part, "tensor")
    residual = inputs + attn_full
    normed_mid, second_back = jax.vjp(layer_norm, residual, second_gain, second_shift)
    mid_low = normed_mid.astype(jnp.bfloat16)
    router_logits = jnp.dot(mid_low, router_weight, preferred_element_type=jnp.float32)
    mixing_logits = jnp.dot(mid_low, mixing_weight, preferred_element_type=jnp.float32)
    chosen = routes[:, None] == lax.iota(jnp.int32, expert_count)[None, :]

    def gating(route_logits, mix_logits):
        router_probs = jax.nn.softmax(route_logits, axis=-1)
        return (
            jnp.sum(jnp.where(chosen, router_probs, 0.0), axis=-1),
            jax.nn.softmax(mix_logits, axis=-1),
        )

    (gate_value, mixing), gating_back = jax.vjp(gating, router_logits, mixing_logits)
    slot_total = expert_count * capacity
    slot_place = jnp.where(slot_index < capacity, routes * capacity + slot_index, slot_total)
    holder = (
        jnp.full((slot_total,), row_count, jnp.int32)
        .at[slot_place]
        .set(lax.iota(jnp.int32, row_count), mode="drop")
    )

    def to_slots(row_values):
        taken = jnp.take(row_values, holder, axis=0, mode="fill", fill_value=0)
        return taken.reshape(expert_count, capacity, row_values.shape[1])

    def from_slots(buffer):
        return jnp.take(
            buffer.reshape(slot_total, buffer.shape[-1]),
            slot_place,
            axis=0,
            mode="fill",
            fill_value=0,
        )

    arrived = lax.all_to_all(to_slots(mid_low), "expert", split_axis=0, concat_axis=1, tiled=True)
    expert_pre = jnp.einsum("erd,edf->erf", arrived, expert_up, preferred_element_type=jnp.float32)
    expert_hidden = gelu_tanh(expert_pre).astype(jnp.bfloat16)
    expert_part = jnp.einsum(
        "erf,efd->erd", expert_hidden, expert_down, preferred_element_type=jnp.float32
    )
    dense_pre = jnp.dot(mid_low, dense_up, preferred_element_type=jnp.float32)
    dense_hidden = gelu_tanh(dense_pre).astype(jnp.bfloat16)
    dense_part = jnp.dot(dense_hidden, dense_down, preferred_element_type=jnp.float32)
    dense_weight = mixing[:, 0:1]
    expert_weight = (mixing[:, 1] * gate_value)[:, None]
    dense_full, expert_full = (
        lax.psum(dense_part.astype(jnp.bfloat16), "tensor").astype(jnp.float32),
        lax.psum(expert_part.astype(jnp.bfloat16), "tensor").astype(jnp.float32),
    )
    expert_tok = from_slots(send_home(expert_full))
    layer_out = residual + dense_weight * dense_full + expert_weight * expert_tok
    dense_dot = jnp.sum(cotan_rows * dense_full, axis=-1)
    expert_dot = jnp.sum(cotan_rows * expert_tok, axis=-1)
    dense_out_grad = (cotan_rows * dense_weight).astype(jnp.bfloat16)
    expert_tok_grad = (cotan_rows * expert_weight).astype(jnp.bfloat16)
    mixing_dots = jnp.stack([dense_dot, gate_value * expert_dot], axis=-1)
    gate_grad = mixing[:, 1] * expert_dot
    router_logit_grad, mixing_logit_grad = gating_back((gate_grad, mixing_dots))
    router_low = router_logit_grad.astype(jnp.bfloat16)
    mixing_low = mixing_logit_grad.astype(jnp.bfloat16)
    router_grad = jnp.einsum("td,te->de", mid_low, router_low, preferred_element_type=jnp.float32)
    mixing_grad = jnp.einsum("td,te->de", mid_low, mixing_low, preferred_element_type=jnp.float32)
    mid_from_gates = jnp.einsum(
        "te,de->td", router_low, router_weight, preferred_element_type=jnp.float32
    ) + jnp.einsum("te,de->td", mixing_low, mixing_weight, preferred_element_type=jnp.float32)
    dense_down_grad = jnp.einsum(
        "tf,td->fd", dense_hidden, dense_out_grad, preferred_element_type=jnp.float32
    )
    dense_hidden_grad = jnp.einsum(
        "td,fd->tf", dense_out_grad, dense_down, preferred_element_type=jnp.float32
    )
    dense_pre_grad = gelu_back(dense_pre, dense_hidden_grad).astype(jnp.bfloat16)
    dense_up_grad = jnp.einsum(
        "td,tf->df", mid_low, dense_pre_grad, preferred_element_type=jnp.float32
    )
    mid_dense_part = jnp.einsum(
        "tf,df->td", dense_pre_grad, dense_up, preferred_element_type=jnp.float32
    )
    grad_arrived = lax.all_to_all(
        to_slots(expert_tok_grad), "expert", split_axis=0, concat_axis=1, tiled=True
    )
    expert_down_grad = jnp.einsum(
        "erf,erd->efd", expert_hidden, grad_arrived, preferred_element_type=jnp.float32
    )
    expert_hidden_grad = jnp.einsum(
        "erd,efd->erf", grad_arrived, expert_down, preferred_element_type=jnp.float32
    )
    expert_pre_grad = gelu_back(expert_pre, expert_hidden_grad).astype(jnp.bfloat16)
    expert_up_grad = jnp.einsum(
        "erd,erf->edf", arrived, expert_pre_grad, preferred_element_type=jnp.float32
    )
    arrived_grad = jnp.einsum(
        "erf,edf->erd", expert_pre_grad, expert_up, preferred_element_type=jnp.float32
    )
    mid_dense, arrived_full = (
        lax.psum(mid_dense_part.astype(jnp.bfloat16), "tensor").astype(jnp.float32),
        lax.psum(arrived_grad.astype(jnp.bfloat16), "tensor").astype(jnp.float32),
    )
    mid_grad = mid_dense + from_slots(send_grads_home(arrived_full)) + mid_from_gates
    resid_from_mid, second_gain_grad, second_shift_grad = second_back(mid_grad)
    residual_grad = cotan_rows + resid_from_mid
    attn_grad_low = residual_grad.astype(jnp.bfloat16)
    project_out_grad = jnp.einsum(
        "tn,td->nd", attended, attn_grad_low, preferred_element_type=jnp.float32
    )
    attended_grad = jnp.einsum(
        "td,nd->tn", attn_grad_low, project_out, preferred_element_type=jnp.float32
    ).astype(jnp.bfloat16)
    qkv_grad = attend_backward(
        queries,
        key_rows,
        values,
        log_total,
        attended_grad.reshape(row_count, head_count, HEAD_DIM),
        block_rows,
    ).astype(jnp.bfloat16)
    project_in_grad = jnp.einsum(
        "td,tcn->dcn", normed_low, qkv_grad, preferred_element_type=jnp.float32
    )
    normed_part = jnp.einsum(
        "tcn,dcn->td", qkv_grad, project_in, preferred_element_type=jnp.float32
    )
    normed_grad = lax.psum(normed_part.astype(jnp.bfloat16), "tensor").astype(jnp.float32)
    input_from_norm, first_gain_grad, first_shift_grad = first_back(normed_grad)
    input_grad = (residual_grad + input_from_norm).astype(jnp.bfloat16)
    (
        router_grad,
        mixing_grad,
        dense_up_grad,
        dense_down_grad,
        second_gain_grad,
        second_shift_grad,
        project_out_grad,
        project_in_grad,
        first_gain_grad,
        first_shift_grad,
    ) = (
        lax.psum(router_grad.astype(jnp.bfloat16), "expert").astype(jnp.float32),
        lax.psum(mixing_grad.astype(jnp.bfloat16), "expert").astype(jnp.float32),
        lax.psum(dense_up_grad.astype(jnp.bfloat16), "expert").astype(jnp.float32),
        lax.psum(dense_down_grad.astype(jnp.bfloat16), "expert").astype(jnp.float32),
        lax.psum(second_gain_grad.astype(jnp.bfloat16), "expert").astype(jnp.float32),
        lax.psum(second_shift_grad.astype(jnp.bfloat16), "expert").astype(jnp.float32),
        lax.psum(project_out_grad.astype(jnp.bfloat16), "expert").astype(jnp.float32),
        lax.psum(project_in_grad.astype(jnp.bfloat16), "expert").astype(jnp.float32),
        lax.psum(first_gain_grad.astype(jnp.bfloat16), "expert").astype(jnp.float32),
        lax.psum(first_shift_grad.astype(jnp.bfloat16), "expert").astype(jnp.float32),
    )
    return (
        layer_out.astype(jnp.bfloat16),
        input_grad,
        first_gain_grad,
        first_shift_grad,
        project_in_grad,
        project_out_grad,
        second_gain_grad,
        second_shift_grad,
        router_grad,
        mixing_grad,
        dense_up_grad,
        dense_down_grad,
        expert_up_grad,
        expert_down_grad,
    )


def solution(mesh):
    placed = (
        P("expert", None),
        P("expert", None),
        P("expert"),
        P("expert"),
        P(),
        P(),
        P(None, None, "tensor"),
        P("tensor", None),
        P(),
        P(),
        P(),
        P(),
        P(None, "tensor"),
        P("tensor", None),
        P("expert", None, "tensor"),
        P("expert", "tensor", None),
    )
    return jax.shard_map(
        local,
        mesh=mesh,
        in_specs=placed,
        out_specs=(
            P("expert", None),
            P("expert", None),
            P(),
            P(),
            P(None, None, "tensor"),
            P("tensor", None),
            P(),
            P(),
            P(),
            P(),
            P(None, "tensor"),
            P("tensor", None),
            P("expert", None, "tensor"),
            P("expert", "tensor", None),
        ),
        check_vma=False,
    )
```

profile of v0, /device:TPU:0, one launch (start us, length us, event | category | flops | bytes accessed | tf_op | source)
XLA Modules:
  0.0 1272.1 jit_solution(15387023293925295045)
XLA Ops:
  16.1 23.0 %while.43 = (s32[]{:T(128)}, bf16[2,512,4,64]{1,3,2,0:T(8,128)(2,1)}, f32[2,4,512]{2,1,0:T(4,128)S(1)}, s32[2]{0:T(128)S(1)}, bf16[1024,4,64]{0,2,1:T(8,128)(2,1...) while((s32[]{:T(128)}, ...), condition=%wide.region_5.6_spmd, body=%wide.region_2.5_spmd.sunk | while | flops 562690560 | bytes 35197428 | solution.py:55
  41.9 3.8 fusion.104
  46.4 4.5 scatter_custom_fusion
  50.9 152.7 %all-reduce.10.cloned.1.call-done = f32[1024,1024]{1,0:T(8,128)} async-done(((f32[1024,1024]{1,0:T(8,128)}), f32[1024,1024]{1,0:T(8,128)}) %all-reduce.10.cloned.1.call-update) | async-done | bytes 4194320 | tf_op jit(solution)/shard_map/psum | solution.py:168
  203.6 3.3 fusion.99
  211.6 12.8 %gather_fusion = bf16[2048,1024]{1,0:T(8,128)(2,1)} fusion(bf16[1024,1024]{1,0:T(8,128)(2,1)} %add_convert_fusion.1, s32[2048]{0:T(1024)S(1)} %fusion.86), kind=kCustom, calls=%fused_computation.clone | custom fusion | bytes 8396800 | tf_op jit(solution)/shard_map/jit(_take)/gather | solution.py:193
  224.4 3.8 broadcast_select_fusion.1
  228.2 4.6 all-to-all-start
  232.8 4.6 fusion.105
  239.4 4.0 convolution_convert_fusion.5
  243.4 38.5 %all-to-all-done = bf16[16,128,1024]{2,1,0:T(8,128)(2,1)} async-done(((bf16[16,128,1024]{2,1,0:T(8,128)(2,1)}), bf16[16,128,1024]{2,1,0:T(8,128)(2,1)}, u32[]{:S(2)}, u32[]{:S(2)}) %all-to-all-start) | async-done | bytes 4194336 | tf_op jit(solution)/shard_map/all_to_all | solution.py:205
  286.7 4.5 fusion.106
  291.2 3.4 copy-done.81
  294.6 6.8 convolution_convert_fusion.1
  301.4 220.2 %all-reduce.18.cloned.1.call-done = (bf16[1024,1024]{1,0:T(8,128)(2,1)}, bf16[2,1024,1024]{2,1,0:T(8,128)(2,1)}) async-done(((bf16[1024,1024]{1,0:T(8,128)(2,1)}, bf16[2,1024,1024]{2,1,0:T(8,128)(2,1)}), (bf16[1024,1024]{1,0:T(8,128)(2,1)}, bf16[2,1024,1024]{2,1,0:T(8,128)(2,1)})) %all-reduce.18.cloned.1.call-update) | async-done | bytes 6291472 | tf_op jit(solution)/shard_map/psum | solution.py:217
  521.6 8.5 copy.55
  530.2 4.7 all-to-all-start.1
  539.6 44.4 %all-to-all-done.1 = bf16[2,1024,1024]{2,0,1:T(2,128)(2,1)} async-done(((bf16[2,1024,1024]{2,0,1:T(2,128)(2,1)}), bf16[2,1024,1024]{2,0,1:T(2,128)(2,1)}, u32[]{:S(2)}, u32[]{:S(2)}) %all-to-all-start.1) | async-done | bytes 4194336 | tf_op jit(solution)/shard_map/all_to_all | solution.py:122
  584.0 7.1 copy.56
  591.1 9.7 gather_fusion.1
  600.8 4.5 fusion.68
  607.2 12.8 %gather_fusion.2 = bf16[2048,1024]{1,0:T(8,128)(2,1)} fusion(bf16[1024,1024]{1,0:T(8,128)(2,1)} %fusion.66, s32[2048]{0:T(1024)S(1)} %fusion.86), kind=kCustom, calls=%fused_computation.2.clone | custom fusion | bytes 8396800 | tf_op jit(solution)/shard_map/jit(_take)/gather | solution.py:193
  620.0 3.8 broadcast_select_fusion
  623.8 4.6 all-to-all-start.2
  628.5 7.7 fusion.62
  637.6 3.7 convolution_convert_fusion.4
  641.3 36.3 %all-to-all-done.2 = bf16[16,128,1024]{2,1,0:T(8,128)(2,1)} async-done(((bf16[16,128,1024]{2,1,0:T(8,128)(2,1)}), bf16[16,128,1024]{2,1,0:T(8,128)(2,1)}, u32[]{:S(2)}, u32[]{:S(2)}) %all-to-all-start.2) | async-done | bytes 4194336 | tf_op jit(solution)/shard_map/all_to_all | solution.py:249
  681.0 12.1 fusion.43
  695.1 6.2 convolution_convert_fusion
  701.3 220.1 %all-reduce.16.cloned.1.call-done = (bf16[2,1024,1024]{2,1,0:T(8,128)(2,1)}, bf16[1024,1024]{1,0:T(8,128)(2,1)}) async-done(((bf16[2,1024,1024]{2,1,0:T(8,128)(2,1)}, bf16[1024,1024]{1,0:T(8,128)(2,1)}), (bf16[2,1024,1024]{2,1,0:T(8,128)(2,1)}, bf16[1024,1024]{1,0:T(8,128)(2,1)})) %all-reduce.16.cloned.1.call-update) | async-done | bytes 6291472 | tf_op jit(solution)/shard_map/psum | solution.py:267
  921.5 8.5 copy.58
  930.0 4.7 all-to-all-start.3
  939.6 44.2 %all-to-all-done.3 = bf16[2,1024,1024]{2,0,1:T(2,128)(2,1)} async-done(((bf16[2,1024,1024]{2,0,1:T(2,128)(2,1)}), bf16[2,1024,1024]{2,0,1:T(2,128)(2,1)}, u32[]{:S(2)}, u32[]{:S(2)}) %all-to-all-start.3) | async-done | bytes 4194336 | tf_op jit(solution)/shard_map/all_to_all | solution.py:128
  983.8 7.1 copy.59
  990.9 9.8 gather_fusion.3
  1000.8 7.5 multiply_reduce_fusion.1
  1009.0 3.6 fusion.98
  1016.7 33.2 %while.44 = (s32[]{:T(128)}, f32[1024,4,64]{0,2,1:T(8,128)}, f32[1024,4,64]{0,2,1:T(8,128)}, bf16[2,512,4,64]{1,3,2,0:T(8,128)(2,1)}, s32[2]{0:T(128)S(1)}, /*in...) while((s32[]{:T(128)}, f32[1024,4,64]{0,2,1:T(8,128)}, ...), condition=%wide.region_27.30_spmd.clone, body=%wide.region_25.29_spmd.clone.sunk | while | flops 1375599104 | bytes 97579512 | solution.py:102
  1057.6 4.9 bitcast_convert_fusion
  1063.0 5.5 convolution_convert_fusion.3
  1068.5 4.4 convolution_convert_fusion.2
  1077.9 13.6 %fusion.97 = f32[2,1024,1024]{2,1,0:T(8,128)} fusion(bf16[2,1024,1024]{2,1,0:T(8,128)(2,1)} %bitcast.152, f32[2,1024,1024]{2,1,0:T(8,128)} %copy-done.81), kind=kOutput, calls=%fused_computation.170 | convolution fusion | flops 4313841664 | bytes 20971520 | tf_op jit(solution)/shard_map/erf,erd->efd/dot_general | solution.py:252
  1091.5 6.9 fusion.107
  1098.4 47.4 %all-reduce.12.cloned.1.call-done = bf16[1024,1024]{1,0:T(8,128)(2,1)} async-done(((bf16[1024,1024]{1,0:T(8,128)(2,1)}), bf16[1024,1024]{1,0:T(8,128)(2,1)}) %all-reduce.12.cloned.1.call-update) | async-done | bytes 2097168 | tf_op jit(solution)/shard_map/psum | solution.py:293
  1153.4 26.6 %all-reduce = (bf16[1024]{0:T(1024)(128)(2,1)S(1)}, bf16[1024]{0:T(1024)(128)(2,1)S(1)}, bf16[1024]{0:T(1024)(128)(2,1)S(1)}, bf16[1024]{0:T(1024)(128)(2,1)S(1)...) all-reduce(bf16[1024]{0:T(1024)(128)(2,1)S(1)} %get-tuple-element.3, ...), channel_id=1, replica_groups=mesh['expert'=8,'tensor'=4] {'expert'}, use_global_device_ids=true, to_apply=%region_32.35 | all-reduce | flops 22528 | bytes 90112 | tf_op jit(solution)/shard_map/psum | solution.py:316
  1183.6 5.5 add_convert_fusion
  1189.1 65.5 %all-reduce.14.cloned.1.call-done = (bf16[1024,3,256]{2,0,1:T(8,128)(2,1)}, bf16[256,1024]{1,0:T(8,128)(2,1)}, bf16[1024,1024]{1,0:T(8,128)(2,1)}, bf16[1024,1024]{1,0:T(8,128)(2,1)}) async-done(((bf16[1024,3,256]{2,0,1:T(8,128)(2,1)}, bf16[256,1024]{1,0:T(8,128)(2,1)}, bf16[1024,1024]{1,0:T(8,128)(2,1)}, bf16[1024,1024]{1,0:T(8,128)(2,1)}), (bf16[1024,3,256]{2,0,1:T(8,128)(2,1)}, ...) | async-done | bytes 6291472 | tf_op jit(solution)/shard_map/psum | solution.py:315
  1256.9 3.3 convert_element_type.230
  (305 shorter events, 123.2 us)
Async XLA Ops:
  7.2 232.2 %copy-start = (bf16[1024,1024]{1,0:T(8,128)(2,1)S(1)}, bf16[1024,1024]{1,0:T(8,128)(2,1)}, u32[]{:S(2)}) copy-start(bf16[1024,1024]{1,0:T(8,128)(2,1)} %param.37) | copy-start | bytes 6291460
  7.2 5.8 copy-start.55
  7.2 5.7 copy-start.77
  7.2 196.4 %all-reduce.10.cloned.1.call-start = ((), (), s32[]{:S(2)}) async-start(), calls=%async_computation.4 | async-start | bytes 8388608 | tf_op jit(solution)/shard_map/psum | solution.py:168
  7.3 5.7 copy-start.9
  7.3 5.7 copy-start.76
  9.4 5.8 copy-start.44
  39.0 6.6 copy-start.3
  39.0 6.6 copy-start.11
  39.1 6.6 copy-start.46
  207.6 16.8 %copy-start.63 = (f32[1024]{0:T(1024)}, f32[1024]{0:T(1024)S(1)}, u32[]{:S(2)}) copy-start(f32[1024]{0:T(1024)S(1)} %multiply_reduce_fusion.3) | copy-start | bytes 12292
  228.2 53.7 %all-to-all-start = ((bf16[16,128,1024]{2,1,0:T(8,128)(2,1)}), bf16[16,128,1024]{2,1,0:T(8,128)(2,1)}, u32[]{:S(2)}, u32[]{:S(2)}) async-start(bf16[16,128,1024]{2,1,0:T(8,128)(2,1)} %bitcast.148), calls=%async_computation | async-start | bytes 8388608 | tf_op jit(solution)/shard_map/all_to_all | solution.py:205
  232.8 288.9 %all-reduce.18.cloned.1.call-start = ((), (), s32[]{:S(2)}) async-start(), calls=%async_computation.8 | async-start | bytes 12582912 | tf_op jit(solution)/shard_map/psum | solution.py:217
  286.7 7.9 copy-start.71
  530.2 7.1 copy-start.42
  530.2 53.8 %all-to-all-start.1 = ((bf16[2,1024,1024]{2,0,1:T(2,128)(2,1)}), bf16[2,1024,1024]{2,0,1:T(2,128)(2,1)}, u32[]{:S(2)}, u32[]{:S(2)}) async-start(bf16[2,1024,1024]{2,0,1:T(2,128)(2,1)} %copy.55), calls=%async_computation.1 | async-start | bytes 8388608 | tf_op jit(solution)/shard_map/all_to_all | solution.py:122
  623.8 53.7 %all-to-all-start.2 = ((bf16[16,128,1024]{2,1,0:T(8,128)(2,1)}), bf16[16,128,1024]{2,1,0:T(8,128)(2,1)}, u32[]{:S(2)}, u32[]{:S(2)}) async-start(bf16[16,128,1024]{2,1,0:T(8,128)(2,1)} %bitcast.147), calls=%async_computation.2 | async-start | bytes 8388608 | tf_op jit(solution)/shard_map/all_to_all | solution.py:249
  628.4 293.0 %all-reduce.16.cloned.1.call-start = ((), (), s32[]{:S(2)}) async-start(), calls=%async_computation.7 | async-start | bytes 12582912 | tf_op jit(solution)/shard_map/psum | solution.py:267
  628.5 9.1 copy-start.75
  680.4 12.7 copy-start.24
  681.0 14.1 %copy-start.74 = (bf16[2,1024,1024]{2,1,0:T(8,128)(2,1)S(1)}, bf16[2,1024,1024]{2,1,0:T(8,128)(2,1)}, u32[]{:S(2)}) copy-start(bf16[2,1024,1024]{2,1,0:T(8,128)(2,1)} %param.38) | copy-start | bytes 12582916
  930.0 53.8 %all-to-all-start.3 = ((bf16[2,1024,1024]{2,0,1:T(2,128)(2,1)}), bf16[2,1024,1024]{2,0,1:T(2,128)(2,1)}, u32[]{:S(2)}, u32[]{:S(2)}) async-start(bf16[2,1024,1024]{2,0,1:T(2,128)(2,1)} %copy.58), calls=%async_computation.3 | async-start | bytes 8388608 | tf_op jit(solution)/shard_map/all_to_all | solution.py:128
  934.7 211.2 %all-reduce.12.cloned.1.call-start = ((), (), s32[]{:S(2)}) async-start(), calls=%async_computation.5 | async-start | bytes 4194304 | tf_op jit(solution)/shard_map/psum | solution.py:293
  990.9 9.8 copy-start.49
  990.9 9.8 copy-start.51
  990.9 9.8 copy-start.54
  1000.7 7.6 copy-start.64
  1000.7 7.6 copy-start.6
  1000.7 7.7 copy-start.13
  1000.7 8.3 copy-start.21
  1062.5 192.2 %all-reduce.14.cloned.1.call-start = ((), (), s32[]{:S(2)}) async-start(), calls=%async_computation.6 | async-start | bytes 12582912 | tf_op jit(solution)/shard_map/psum | solution.py:315
  1062.9 5.5 copy-start.17
  1068.4 6.0 copy-start.10
  1068.4 6.0 copy-start.38
  1068.4 6.0 copy-start.39
  1068.5 6.0 copy-start.45
  1068.5 6.0 copy-start.56
  1068.5 6.0 copy-start.58
  1068.5 6.0 copy-start.78
  1077.8 13.7 %copy-start.23 = (bf16[2,8,128,1024]{3,2,1,0:T(8,128)(2,1)S(1)}, bf16[2,8,128,1024]{3,2,1,0:T(8,128)(2,1)}, u32[]{:S(2)}) copy-start(bf16[2,8,128,1024]{3,2,1,0:T(8,128)(2,1)} %copy-done.22) | copy-start | bytes 12582916
  1077.9 13.6 %copy-start.83 = (bf16[2,1024,1024]{2,1,0:T(8,128)(2,1)S(1)}, bf16[2,1024,1024]{2,1,0:T(8,128)(2,1)}, u32[]{:S(2)}) copy-start(bf16[2,1024,1024]{2,1,0:T(8,128)(2,1)} %copy-done.82) | copy-start | bytes 12582916
  1098.4 52.2 %copy-start.62 = (f32[1024]{0:T(1024)S(1)}, f32[1024]{0:T(1024)}, u32[]{:S(2)}) copy-start(f32[1024]{0:T(1024)} %copy-done.61) | copy-start | bytes 12292
  1147.8 5.5 copy-start.43
  1147.9 5.5 copy-start.65
  1147.9 5.5 copy-start.67
  1147.9 5.5 copy-start.68
  1147.9 35.8 %copy-start.60 = (f32[1024]{0:T(1024)S(1)}, f32[1024]{0:T(1024)}, u32[]{:S(2)}) copy-start(f32[1024]{0:T(1024)} %copy-done.59) | copy-start | bytes 12292
  1254.7 5.6 copy-start.29
  (57 other events, 132.2 us)
Sparse Core Ops, SparseCore 0:
  45.9 157.6 all-reduce.9
  301.6 220.0 all-reduce.17
  701.5 219.9 all-reduce.15
  1062.6 83.2 all-reduce.11
  1150.5 104.1 all-reduce.13
where the time goes:
time: 1280 us; the launch traced here: 1270 us
  waiting for transfers between devices  869 us (68%)
  matrix products  142 us (11%)
  local copies, waits for them, and re-layouts  119 us (9%)
  other arithmetic  69.5 us (5%)
  blocking collectives  26.6 us (2%)
  starting transfers between devices  19.2 us (2%)
  between operations  14.9 us (1%)
    psum x1, waiting for transfers between devices, local(): lax.psum(dense_part.astype(jnp.bfloat16), 'tensor').astype(jnp.float32)  220 us
    psum x1, waiting for transfers between devices, local(): lax.psum(arrived_grad.astype(jnp.bfloat16), 'tensor').astype(jnp.float32)  220 us
    psum x1, waiting for transfers between devices, local(): attn_full = lax.psum(attn_part, 'tensor')  153 us
    psum x1, waiting for transfers between devices, local(): lax.psum(project_in_grad.astype(jnp.bfloat16), 'expert').astype(jnp.float32)  65.5 us
    psum x1, waiting for transfers between devices, local(): lax.psum(normed_part.astype(jnp.bfloat16), 'tensor').astype(jnp.float32)  47.4 us
    all_to_all x1, waiting for transfers between devices, send_home(): lax.all_to_all(buffer.astype(jnp.bfloat16), 'expert', split_axis=1, conca...  44.4 us
    all_to_all x1, waiting for transfers between devices, send_grads_home(): lax.all_to_all(buffer.astype(jnp.bfloat16), 'expert', split_axis=1, conca...  44.2 us
    all_to_all x1, waiting for transfers between devices, local(): lax.all_to_all(to_slots(mid_low), 'expert', split_axis=0, concat_axis=1,...  38.5 us
  transfers between devices with their start and end apart: 9, of which 9 were waited for; matrix products, arithmetic and copies ran while one was open for 7% of the time, Pallas kernels for 0%

commit v1 on v0

--- a/solution.py
+++ b/solution.py
@@ -7,6 +7,10 @@
 SEQ = 1024
 EPS = 1e-05
 NEGATIVE = -1e30
+
+
+def process_teams_up(vec):
+    return jnp.sum(jax.lax.all_gather(vec, "expert"), axis=0)
 
 
 def layer_norm(row_values, norm_gain, norm_shift):
@@ -312,7 +316,7 @@
         lax.psum(second_gain_grad.astype(jnp.bfloat16), "expert").astype(jnp.float32),
         lax.psum(second_shift_grad.astype(jnp.bfloat16), "expert").astype(jnp.float32),
         lax.psum(project_out_grad.astype(jnp.bfloat16), "expert").astype(jnp.float32),
-        lax.psum(project_in_grad.astype(jnp.bfloat16), "expert").astype(jnp.float32),
+        process_teams_up(project_in_grad.astype(jnp.bfloat16)).astype(jnp.float32),
         lax.psum(first_gain_grad.astype(jnp.bfloat16), "expert").astype(jnp.float32),
         lax.psum(first_shift_grad.astype(jnp.bfloat16), "expert").astype(jnp.float32),
     )

time: 1280 us -> 1330 us (1.039)
  waiting for transfers between devices: 869 us -> 919 us
    all_gather x0 -> x1, waiting for transfers between devices: none -> 65 us  [process_teams_up(): return jnp.sum(jax.lax.all_gather(vec, 'expert'), axis=0)]
    psum x1, waiting for transfers between devices: 65.5 us -> 48.2 us  [local(): lax.psum(project_out_grad.astype(jnp.bfloat16), 'expert')]
  transfers between devices with their start and end apart: 9 -> 10, of which waited for: 9 -> 10; matrix products, arithmetic and copies ran while one was open for 7% -> 7% of each run, Pallas kernels for 0% -> 0%
where the time goes in v1:
time: 1330 us; the launch traced here: 1320 us
  waiting for transfers between devices  919 us (69%)
  matrix products  140 us (11%)
  local copies, waits for them, and re-layouts  119 us (9%)
  other arithmetic  76.4 us (6%)
  blocking collectives  26.3 us (2%)
  starting transfers between devices  18.6 us (1%)
  between operations  15.4 us (1%)
    psum x1, waiting for transfers between devices, local(): lax.psum(dense_part.astype(jnp.bfloat16), 'tensor').astype(jnp.float32)  220 us
    psum x1, waiting for transfers between devices, local(): lax.psum(arrived_grad.astype(jnp.bfloat16), 'tensor').astype(jnp.float32)  220 us
    psum x1, waiting for transfers between devices, local(): attn_full = lax.psum(attn_part, 'tensor')  153 us
    all_gather x1, waiting for transfers between devices, process_teams_up(): return jnp.sum(jax.lax.all_gather(vec, 'expert'), axis=0)  65 us
    psum x1, waiting for transfers between devices, local(): lax.psum(project_out_grad.astype(jnp.bfloat16), 'expert')  48.2 us
    psum x1, waiting for transfers between devices, local(): lax.psum(normed_part.astype(jnp.bfloat16), 'tensor').astype(jnp.float32)  47.2 us
    all_to_all x1, waiting for transfers between devices, send_grads_home(): lax.all_to_all(buffer.astype(jnp.bfloat16), 'expert', split_axis=1, conca...  46.1 us
    all_to_all x1, waiting for transfers between devices, send_home(): lax.all_to_all(buffer.astype(jnp.bfloat16), 'expert', split_axis=1, conca...  44.4 us
  transfers between devices with their start and end apart: 10, of which 10 were waited for; matrix products, arithmetic and copies ran while one was open for 7% of the time, Pallas kernels for 0%

profile of v1, /device:TPU:0, one launch (start us, length us, event | category | flops | bytes accessed | tf_op | source)
XLA Modules:
  0.0 1324.9 jit_solution(3342364887834271914)
XLA Ops:
  16.1 23.0 %while.43 = (s32[]{:T(128)}, bf16[2,512,4,64]{1,3,2,0:T(8,128)(2,1)}, f32[2,4,512]{2,1,0:T(4,128)S(1)}, s32[2]{0:T(128)S(1)}, bf16[1024,4,64]{0,2,1:T(8,128)(2,1...) while((s32[]{:T(128)}, ...), condition=%wide.region_5.6_spmd, body=%wide.region_2.5_spmd.sunk | while | flops 562690560 | bytes 35197428 | solution.py:59
  41.9 3.8 fusion.104
  46.4 4.5 scatter_custom_fusion
  50.9 152.7 %all-reduce.10.cloned.1.call-done = f32[1024,1024]{1,0:T(8,128)} async-done(((f32[1024,1024]{1,0:T(8,128)}), f32[1024,1024]{1,0:T(8,128)}) %all-reduce.10.cloned.1.call-update) | async-done | bytes 4194320 | tf_op jit(solution)/shard_map/psum | solution.py:172
  211.6 12.8 gather_fusion
  224.4 3.8 broadcast_select_fusion.1
  228.2 4.6 all-to-all-start
  232.8 4.5 fusion.105
  239.4 4.0 convolution_convert_fusion.5
  243.3 38.5 %all-to-all-done = bf16[16,128,1024]{2,1,0:T(8,128)(2,1)} async-done(((bf16[16,128,1024]{2,1,0:T(8,128)(2,1)}), bf16[16,128,1024]{2,1,0:T(8,128)(2,1)}, u32[]{:S(2)}, u32[]{:S(2)}) %all-to-all-start) | async-done | bytes 4194336 | tf_op jit(solution)/shard_map/all_to_all | solution.py:209
  286.7 4.5 fusion.106
  294.4 6.8 convolution_convert_fusion.1
  301.3 220.2 %all-reduce.18.cloned.1.call-done = (bf16[1024,1024]{1,0:T(8,128)(2,1)}, bf16[2,1024,1024]{2,1,0:T(8,128)(2,1)}) async-done(((bf16[1024,1024]{1,0:T(8,128)(2,1)}, bf16[2,1024,1024]{2,1,0:T(8,128)(2,1)}), (bf16[1024,1024]{1,0:T(8,128)(2,1)}, bf16[2,1024,1024]{2,1,0:T(8,128)(2,1)})) %all-reduce.18.cloned.1.call-update) | async-done | bytes 6291472 | tf_op jit(solution)/shard_map/psum | solution.py:221
  521.5 8.5 copy.55
  530.0 4.7 all-to-all-start.1
  539.4 44.4 %all-to-all-done.1 = bf16[2,1024,1024]{2,0,1:T(2,128)(2,1)} async-done(((bf16[2,1024,1024]{2,0,1:T(2,128)(2,1)}), bf16[2,1024,1024]{2,0,1:T(2,128)(2,1)}, u32[]{:S(2)}, u32[]{:S(2)}) %all-to-all-start.1) | async-done | bytes 4194336 | tf_op jit(solution)/shard_map/all_to_all | solution.py:126
  583.8 7.1 copy.56
  591.0 9.7 gather_fusion.1
  600.7 4.5 fusion.68
  607.1 12.8 gather_fusion.2
  619.8 3.8 broadcast_select_fusion
  623.7 4.6 all-to-all-start.2
  628.3 7.7 fusion.62
  637.3 3.7 convolution_convert_fusion.4
  641.0 36.3 %all-to-all-done.2 = bf16[16,128,1024]{2,1,0:T(8,128)(2,1)} async-done(((bf16[16,128,1024]{2,1,0:T(8,128)(2,1)}), bf16[16,128,1024]{2,1,0:T(8,128)(2,1)}, u32[]{:S(2)}, u32[]{:S(2)}) %all-to-all-start.2) | async-done | bytes 4194336 | tf_op jit(solution)/shard_map/all_to_all | solution.py:253
  680.8 12.1 fusion.43
  694.9 6.2 convolution_convert_fusion
  701.1 220.1 %all-reduce.16.cloned.1.call-done = (bf16[2,1024,1024]{2,1,0:T(8,128)(2,1)}, bf16[1024,1024]{1,0:T(8,128)(2,1)}) async-done(((bf16[2,1024,1024]{2,1,0:T(8,128)(2,1)}, bf16[1024,1024]{1,0:T(8,128)(2,1)}), (bf16[2,1024,1024]{2,1,0:T(8,128)(2,1)}, bf16[1024,1024]{1,0:T(8,128)(2,1)})) %all-reduce.16.cloned.1.call-update) | async-done | bytes 6291472 | tf_op jit(solution)/shard_map/psum | solution.py:271
  921.3 8.5 copy.58
  929.8 4.6 all-to-all-start.3
  937.3 46.1 %all-to-all-done.3 = bf16[2,1024,1024]{2,0,1:T(2,128)(2,1)} async-done(((bf16[2,1024,1024]{2,0,1:T(2,128)(2,1)}), bf16[2,1024,1024]{2,0,1:T(2,128)(2,1)}, u32[]{:S(2)}, u32[]{:S(2)}) %all-to-all-start.3) | async-done | bytes 4194336 | tf_op jit(solution)/shard_map/all_to_all | solution.py:132
  983.5 7.1 copy.59
  990.6 9.8 gather_fusion.3
  1000.5 7.5 multiply_reduce_fusion.1
  1016.8 31.3 %while.44 = (s32[]{:T(128)}, f32[1024,4,64]{0,2,1:T(8,128)S(1)}, f32[1024,4,64]{0,2,1:T(8,128)}, bf16[2,512,4,64]{1,3,2,0:T(8,128)(2,1)}, s32[2]{0:T(128)S(1)}, ...) while((s32[]{:T(128)}, f32[1024,4,64]{0,2,1:T(8,128)S(1)}, ...), condition=%wide.region_27.30_spmd.clone, body=%wide.region_25.29_spmd.clone.sunk | while | flops 1375599104 | bytes 87093672 | solution.py:106
  1053.1 5.1 bitcast_convert_fusion
  1058.3 5.5 convolution_convert_fusion.3
  1063.8 4.4 convolution_convert_fusion.2
  1069.9 5.0 convolution_convert_fusion.6
  1077.2 9.5 fusion.107
  1086.8 7.7 fusion.97
  1094.4 47.2 %all-reduce.12.cloned.1.call-done = bf16[1024,1024]{1,0:T(8,128)(2,1)} async-done(((bf16[1024,1024]{1,0:T(8,128)(2,1)}), bf16[1024,1024]{1,0:T(8,128)(2,1)}) %all-reduce.12.cloned.1.call-update) | async-done | bytes 2097168 | tf_op jit(solution)/shard_map/psum | solution.py:297
  1149.1 26.3 %all-reduce = (bf16[1024]{0:T(1024)(128)(2,1)S(1)}, bf16[1024]{0:T(1024)(128)(2,1)S(1)}, bf16[1024]{0:T(1024)(128)(2,1)S(1)}, bf16[1024]{0:T(1024)(128)(2,1)S(1)...) all-reduce(bf16[1024]{0:T(1024)(128)(2,1)S(1)} %get-tuple-element.3, ...), channel_id=1, replica_groups=mesh['expert'=8,'tensor'=4] {'expert'}, use_global_device_ids=true, to_apply=%region_32.35 | all-reduce | flops 22528 | bytes 90112 | tf_op jit(solution)/shard_map/psum | solution.py:320
  1179.0 5.4 add_convert_fusion
  1184.4 48.2 %all-reduce.14.cloned.1.call-done = (bf16[256,1024]{1,0:T(8,128)(2,1)}, bf16[1024,1024]{1,0:T(8,128)(2,1)}, bf16[1024,1024]{1,0:T(8,128)(2,1)}) async-done(((bf16[256,1024]{1,0:T(8,128)(2,1)}, bf16[1024,1024]{1,0:T(8,128)(2,1)}, bf16[1024,1024]{1,0:T(8,128)(2,1)}), (bf16[256,1024]{1,0:T(8,128)(2,1)}, bf16[1024,1024]{1,0:T(8,128)(2,1)}, bf16[1024,1024]{1,0:T(8,128)(2,1)})) %all-reduce.14.cloned.1.call-update) | async-done | bytes 4718608 | tf_op jit(solution)/shard_map/psum | solution.py:318
  1234.9 4.1 convert_element_type.244
  1241.4 65.0 %all-gather.3.cloned.1.call-done = bf16[8192,3,256]{2,0,1:T(8,128)(2,1)} async-done(((bf16[1024,3,256]{2,0,1:T(8,128)(2,1)}), bf16[8192,3,256]{2,0,1:T(8,128)(2,1)}) %all-gather.3.cloned.1.call-update) | async-done | bytes 12582928 | tf_op jit(solution)/shard_map/all_gather | solution.py:13
  1306.5 8.0 reduce_sum.274
  (322 shorter events, 126.4 us)
Async XLA Ops:
  7.2 232.2 %copy-start = (bf16[1024,1024]{1,0:T(8,128)(2,1)S(1)}, bf16[1024,1024]{1,0:T(8,128)(2,1)}, u32[]{:S(2)}) copy-start(bf16[1024,1024]{1,0:T(8,128)(2,1)} %param.37) | copy-start | bytes 6291460
  7.2 5.8 copy-start.62
  7.2 5.7 copy-start.85
  7.2 196.4 %all-reduce.10.cloned.1.call-start = ((), (), s32[]{:S(2)}) async-start(), calls=%async_computation.4 | async-start | bytes 8388608 | tf_op jit(solution)/shard_map/psum | solution.py:172
  7.3 5.7 copy-start.7
  7.3 5.7 copy-start.84
  9.4 5.8 copy-start.44
  39.0 6.6 copy-start.3
  39.0 6.6 copy-start.9
  39.0 6.6 copy-start.50
  228.2 53.7 %all-to-all-start = ((bf16[16,128,1024]{2,1,0:T(8,128)(2,1)}), bf16[16,128,1024]{2,1,0:T(8,128)(2,1)}, u32[]{:S(2)}, u32[]{:S(2)}) async-start(bf16[16,128,1024]{2,1,0:T(8,128)(2,1)} %bitcast.149), calls=%async_computation | async-start | bytes 8388608 | tf_op jit(solution)/shard_map/all_to_all | solution.py:209
  232.8 288.7 %all-reduce.18.cloned.1.call-start = ((), (), s32[]{:S(2)}) async-start(), calls=%async_computation.9 | async-start | bytes 12582912 | tf_op jit(solution)/shard_map/psum | solution.py:221
  286.7 7.7 copy-start.79
  530.0 7.1 copy-start.43
  530.0 53.8 %all-to-all-start.1 = ((bf16[2,1024,1024]{2,0,1:T(2,128)(2,1)}), bf16[2,1024,1024]{2,0,1:T(2,128)(2,1)}, u32[]{:S(2)}, u32[]{:S(2)}) async-start(bf16[2,1024,1024]{2,0,1:T(2,128)(2,1)} %copy.55), calls=%async_computation.1 | async-start | bytes 8388608 | tf_op jit(solution)/shard_map/all_to_all | solution.py:126
  539.4 395.2 %copy-start.30 = (f32[1024,16]{0,1:T(8,128)}, f32[1024,16]{0,1:T(8,128)S(1)}, u32[]{:S(2)}) copy-start(f32[1024,16]{0,1:T(8,128)S(1)} %get-tuple-element.419) | copy-start | bytes 196612
  539.4 395.1 %copy-start.46 = (f32[1024]{0:T(1024)}, f32[1024]{0:T(1024)S(1)}, u32[]{:S(2)}) copy-start(f32[1024]{0:T(1024)S(1)} %get-tuple-element.418) | copy-start | bytes 12292
  539.4 395.1 %copy-start.48 = (f32[1024]{0:T(1024)}, f32[1024]{0:T(1024)S(1)}, u32[]{:S(2)}) copy-start(f32[1024]{0:T(1024)S(1)} %fusion.85) | copy-start | bytes 12292
  605.2 329.3 %copy-start.56 = (f32[1024]{0:T(1024)}, f32[1024]{0:T(1024)S(1)}, u32[]{:S(2)}) copy-start(f32[1024]{0:T(1024)S(1)} %mul.424) | copy-start | bytes 12292
  623.7 53.7 %all-to-all-start.2 = ((bf16[16,128,1024]{2,1,0:T(8,128)(2,1)}), bf16[16,128,1024]{2,1,0:T(8,128)(2,1)}, u32[]{:S(2)}, u32[]{:S(2)}) async-start(bf16[16,128,1024]{2,1,0:T(8,128)(2,1)} %bitcast.148), calls=%async_computation.2 | async-start | bytes 8388608 | tf_op jit(solution)/shard_map/all_to_all | solution.py:253
  628.2 293.0 %all-reduce.16.cloned.1.call-start = ((), (), s32[]{:S(2)}) async-start(), calls=%async_computation.8 | async-start | bytes 12582912 | tf_op jit(solution)/shard_map/psum | solution.py:271
  628.3 9.0 copy-start.83
  680.2 12.7 copy-start.22
  680.8 14.1 %copy-start.82 = (bf16[2,1024,1024]{2,1,0:T(8,128)(2,1)S(1)}, bf16[2,1024,1024]{2,1,0:T(8,128)(2,1)}, u32[]{:S(2)}) copy-start(bf16[2,1024,1024]{2,1,0:T(8,128)(2,1)} %param.38) | copy-start | bytes 12582916
  929.8 53.7 %all-to-all-start.3 = ((bf16[2,1024,1024]{2,0,1:T(2,128)(2,1)}), bf16[2,1024,1024]{2,0,1:T(2,128)(2,1)}, u32[]{:S(2)}, u32[]{:S(2)}) async-start(bf16[2,1024,1024]{2,0,1:T(2,128)(2,1)} %copy.58), calls=%async_computation.3 | async-start | bytes 8388608 | tf_op jit(solution)/shard_map/all_to_all | solution.py:132
  934.4 207.2 %all-reduce.12.cloned.1.call-start = ((), (), s32[]{:S(2)}) async-start(), calls=%async_computation.5 | async-start | bytes 4194304 | tf_op jit(solution)/shard_map/psum | solution.py:297
  934.5 56.1 %copy-start.68 = (f32[1024]{0:T(1024)}, f32[1024]{0:T(1024)S(1)}, u32[]{:S(2)}) copy-start(f32[1024]{0:T(1024)S(1)} %neg.18) | copy-start | bytes 12292
  990.6 9.9 copy-start.53
  990.6 9.9 copy-start.55
  990.6 9.9 copy-start.61
  1000.4 7.6 copy-start.73
  1000.5 7.6 copy-start.6
  1000.5 7.7 copy-start.11
  1000.5 8.3 copy-start.19
  1058.2 174.4 %all-reduce.14.cloned.1.call-start = ((), (), s32[]{:S(2)}) async-start(), calls=%async_computation.7 | async-start | bytes 9437184 | tf_op jit(solution)/shard_map/psum | solution.py:318
  1058.3 5.5 copy-start.15
  1058.3 5.5 copy-start.88
  1069.8 236.7 %all-gather.3.cloned.1.call-start = ((), (), s32[]{:S(2)}) async-start(), calls=%async_computation.6 | async-start | bytes 14155776 | tf_op jit(solution)/shard_map/all_gather | solution.py:13
  1075.0 11.8 slice-start
  1077.2 9.6 copy-start.23
  1077.2 9.6 slice-start.1
  1086.8 56.8 %copy-start.8 = (bf16[1024,1024]{1,0:T(8,128)(2,1)S(1)}, bf16[1024,1024]{1,0:T(8,128)(2,1)}, u32[]{:S(2)}) copy-start(bf16[1024,1024]{1,0:T(8,128)(2,1)} %param.24) | copy-start | bytes 6291460
  1094.4 51.9 %copy-start.71 = (f32[1024]{0:T(1024)S(1)}, f32[1024]{0:T(1024)}, u32[]{:S(2)}) copy-start(f32[1024]{0:T(1024)} %copy-done.70) | copy-start | bytes 12292
  1143.6 5.5 copy-start.75
  1143.6 5.5 copy-start.76
  1143.6 35.4 %copy-start.67 = (f32[1024]{0:T(1024)S(1)}, f32[1024]{0:T(1024)}, u32[]{:S(2)}) copy-start(f32[1024]{0:T(1024)} %copy-done.66) | copy-start | bytes 12292
  1232.6 6.3 copy-start.27
  1306.5 11.3 copy-start.1
  (64 other events, 133.4 us)
Sparse Core Ops, SparseCore 0:
  45.8 157.6 all-reduce.9
  301.4 220.0 all-reduce.17
  701.2 219.9 all-reduce.15
  1058.3 83.2 all-reduce.11
  1145.6 86.9 all-reduce.13
  1234.4 72.0 all-gather.2
